TPU v7x, 32 devices: a whole 2x2x4 slice. The times are simulated.
32 devices in a mesh: fsdp: 16 (over z, x, core), dp: 2 (over y).
Axes of the slice: x: 2, y: 2, z: 4, core: 2. Of those that a mesh axis runs over, the one named last changes fastest.
Arguments:
- inputs: bfloat16 [6144, 4096], P(('fsdp', 'dp')), may hold values from -6 to 6
- grad_out: bfloat16 [6144, 14336], P(('fsdp', 'dp')), may hold values from -0.009765625 to 0.009765625
- projection: bfloat16 [4096, 128], P('fsdp'), may hold values from -0.375 to 0.375
- moment: float32 [14336, 128], P('fsdp'), may hold values from -1.5 to 1.5
- second: float32 [14336, 128], P('fsdp'), may hold values from 0.0001 to 0.001
Outputs:
- update: bfloat16 [4096, 14336], P('fsdp')
- new_moment: float32 [14336, 128], P('fsdp')
- new_second: float32 [14336, 128], P('fsdp')
All inputs are finite; a program needn't handle non-finite values.
Results may differ from a plain program's by a relative error of at most 0.0051.
Values may be sent and summed in bfloat16 or wider, within the bound.
No kernel may reach another device: no remote copies, remote signals or barrier semaphores. Data moves between devices by JAX's collectives and lax.ppermute only.
A program may use at most 64 MiB of HBM per device.

v0:
```python
import jax
import jax.numpy as jnp
from jax import lax
from jax.sharding import PartitionSpec as P

STEP = 10


def adam_step(low_rank, moment, second):
    new_moment = 0.9 * moment + 0.1 * low_rank
    new_second = 0.999 * second + 0.001 * (low_rank * low_rank)
    first_fix = 1.0 - 0.9**STEP
    second_fix = 1.0 - 0.999**STEP
    normalized = (new_moment / first_fix / (jnp.sqrt(new_second / second_fix) + 1e-08)).astype(
        jnp.bfloat16
    )
    return (new_moment, new_second, normalized)


def local(inputs, grad_out, projection, moment, second):
    projected = jnp.dot(
        inputs,
        lax.all_gather(projection, "fsdp", axis=0, tiled=True),
        preferred_element_type=jnp.float32,
    ).astype(jnp.bfloat16)
    contract = (((0,), (0,)), ((), ()))
    whole = lax.dot_general(grad_out, projected, contract, preferred_element_type=jnp.float32)
    whole = lax.psum(whole, "dp")
    low_rank = lax.psum_scatter(whole, "fsdp", scatter_dimension=0, tiled=True)
    new_moment, new_second, normalized = adam_step(low_rank, moment, second)
    expand = (((1,), (1,)), ((), ()))
    update = lax.dot_general(
        projection,
        lax.all_gather(normalized, "fsdp", axis=0, tiled=True),
        expand,
        preferred_element_type=jnp.float32,
    ).astype(jnp.bfloat16)
    return (update, new_moment, new_second)


def solution(mesh):
    in_specs = (
        P(("fsdp", "dp"), None),
        P(("fsdp", "dp"), None),
        P("fsdp", None),
        P("fsdp", None),
        P("fsdp", None),
    )
    out_specs = (P("fsdp", None), P("fsdp", None), P("fsdp", None))
    return jax.shard_map(local, mesh=mesh, in_specs=in_specs, out_specs=out_specs, check_vma=False)
```

profile of v0, /device:TPU:0, one launch (start us, length us, event | category | flops | bytes accessed | tf_op | source)
XLA Modules:
  0.0 252.6 jit_solution(8466995799311963233)
XLA Ops:
  7.2 0.0 copy-start
  7.2 0.0 all-gather.3.cloned.1.call-start
  7.2 0.7 all-gather.3.cloned.1.call-update
  7.9 0.0 reduce-scatter.2.cloned.1.call-start
  8.0 42.8 %all-gather.3.cloned.1.call-done = bf16[4096,128]{1,0:T(8,128)(2,1)} async-done(((bf16[256,128]{1,0:T(8,128)(2,1)}), bf16[4096,128]{1,0:T(8,128)(2,1)}) %all-gather.3.cloned.1.call-update) | async-done | bytes 1048592 | tf_op jit(solution)/shard_map/all_gather | solution.py:23
  50.7 0.0 copy-done
  50.7 7.6 %convolution_bitcast_fusion = f32[14336,128]{0,1:T(8,128)} fusion(bf16[192,14336]{1,0:T(8,128)(2,1)} %param.6, bf16[192,4096]{1,0:T(8,128)(2,1)S(1)} %copy-done, bf16[4096,128]{1,0:T(8,128)(2,1)} %all-gather.3.cloned.1.call-done), kind=kOutput, calls=%fused_computation.2 | convolution fusion | flops 905994240 | bytes 15466496 | tf_op jit(solution)/shard_map/dot_general | solution.py:27
  58.4 0.0 reduce-scatter.2.cloned.1.call-update
  58.4 0.0 all-reduce.2.cloned.1.call-start
  58.5 90.7 %reduce-scatter.2.cloned.1.call-done = f32[896,128]{0,1:T(8,128)} async-done(((f32[14336,128]{0,1:T(8,128)}), f32[896,128]{0,1:T(8,128)}) %reduce-scatter.2.cloned.1.call-update) | async-done | bytes 458768 | tf_op jit(solution)/shard_map/reduce_scatter | solution.py:29
  149.2 0.0 all-reduce.2.cloned.1.call-update
  149.2 0.0 all-gather.5.cloned.1.call-start
  149.3 0.0 copy-done.1
  149.3 0.2 copy.8
  149.5 0.0 copy-done.2
  149.5 0.2 copy.9
  149.7 28.8 %all-reduce.2.cloned.1.call-done = f32[896,128]{0,1:T(8,128)} async-done(((f32[896,128]{0,1:T(8,128)}), f32[896,128]{0,1:T(8,128)}) %all-reduce.2.cloned.1.call-update) | async-done | bytes 458768 | tf_op jit(solution)/shard_map/psum | solution.py:28
  178.5 2.0 divide_convert_fusion
  180.5 0.0 all-gather.5.cloned.1.call-update
  180.5 1.0 copy.11
  181.5 1.0 copy.12
  182.4 46.4 %all-gather.5.cloned.1.call-done = bf16[14336,128]{0,1:T(8,128)(2,1)} async-done(((bf16[896,128]{0,1:T(8,128)(2,1)}), bf16[14336,128]{0,1:T(8,128)(2,1)}) %all-gather.5.cloned.1.call-update) | async-done | bytes 3670032 | tf_op jit(solution)/shard_map/all_gather | solution.py:34
  228.9 7.1 %fusion = bf16[256,14336]{0,1:T(8,128)(2,1)} fusion(bf16[14336,128]{0,1:T(8,128)(2,1)} %all-gather.5.cloned.1.call-done, bf16[256,128]{1,0:T(8,128)(2,1)S(1)} %copy-done.3), kind=kOutput, calls=%fused_computation.1 | convolution fusion | flops 943194112 | bytes 11075584 | tf_op jit(solution)/shard_map/dot_general | solution.py:32
  236.0 10.1 %copy.10 = bf16[256,14336]{1,0:T(8,128)(2,1)} copy(bf16[256,14336]{0,1:T(8,128)(2,1)} %fusion) | data formatting | bytes 14680064
  (4 shorter events, 0.0 us)
Async XLA Ops:
  7.2 43.6 %copy-start = (bf16[192,4096]{1,0:T(8,128)(2,1)S(1)}, bf16[192,4096]{1,0:T(8,128)(2,1)}, u32[]{:S(2)}) copy-start(bf16[192,4096]{1,0:T(8,128)(2,1)} %param.5) | copy-start | bytes 4718596
  7.2 43.6 %all-gather.3.cloned.1.call-start = ((), (), s32[]{:S(2)}) async-start(), calls=%async_computation.1 | async-start | bytes 1114112 | tf_op jit(solution)/shard_map/all_gather | solution.py:23
  7.9 141.3 %reduce-scatter.2.cloned.1.call-start = ((), (), s32[]{:S(2)}) async-start(), calls=%async_computation.3 | async-start | bytes 7798784 | tf_op jit(solution)/shard_map/reduce_scatter | solution.py:29
  58.4 90.9 %copy-start.1 = (f32[896,128]{1,0:T(8,128)S(1)}, f32[896,128]{1,0:T(8,128)}, u32[]{:S(2)}) copy-start(f32[896,128]{1,0:T(8,128)} %param.8) | copy-start | bytes 1376260
  58.4 91.1 %copy-start.2 = (f32[896,128]{1,0:T(8,128)S(1)}, f32[896,128]{1,0:T(8,128)}, u32[]{:S(2)}) copy-start(f32[896,128]{1,0:T(8,128)} %param.9) | copy-start | bytes 1376260
  58.4 170.5 %copy-start.3 = (bf16[256,128]{1,0:T(8,128)(2,1)S(1)}, bf16[256,128]{1,0:T(8,128)(2,1)}, u32[]{:S(2)}) copy-start(bf16[256,128]{1,0:T(8,128)(2,1)} %param.7) | copy-start | bytes 196612
  58.4 120.1 %all-reduce.2.cloned.1.call-start = ((), (), s32[]{:S(2)}) async-start(), calls=%async_computation.4 | async-start | bytes 917504 | tf_op jit(solution)/shard_map/psum | solution.py:28
  149.2 79.6 %all-gather.5.cloned.1.call-start = ((), (), s32[]{:S(2)}) async-start(), calls=%async_computation.2 | async-start | bytes 3899392 | tf_op jit(solution)/shard_map/all_gather | solution.py:34
Sparse Core Ops, SparseCore 0:
  10.1 40.5 all-gather.2
  58.5 90.6 reduce-scatter.1
  151.5 26.9 all-reduce.1
  181.1 47.7 all-gather.4
where the time goes:
time: 253 us
  waiting for transfers between devices  209 us (83%)
  matrix products  14.7 us (6%)
  between operations  13.8 us (5%)
  local copies, waits for them, and re-layouts  12.5 us (5%)
    reduce_scatter x1, waiting for transfers between devices, local(): low_rank = lax.psum_scatter(whole, 'fsdp', scatter_dimension=0, tiled=True)  90.7 us
    all_gather x1, waiting for transfers between devices, local(): lax.all_gather(normalized, 'fsdp', axis=0, tiled=True)  46.4 us
    all_gather x1, waiting for transfers between devices, local(): lax.all_gather(projection, 'fsdp', axis=0, tiled=True)  42.8 us
    psum x1, waiting for transfers between devices, local(): whole = lax.psum(whole, 'dp')  28.8 us
    unnamed x13, local copies, waits for them, and re-layouts  12.5 us
    dot_general x1, matrix products, local(): lax.dot_general(grad_out, projected, contract, preferred_element_type=jnp...  7.64 us
    dot_general x1, matrix products, local(): lax.dot_general(projection, lax.all_gather(normalized, 'fsdp', axis=0, ti...  7.09 us
  transfers between devices with their start and end apart: 4, of which 4 were waited for; matrix products, arithmetic and copies ran while one was open for 1% of the time, Pallas kernels for 0%

commit v1 on v0

--- a/solution.py
+++ b/solution.py
@@ -4,6 +4,19 @@
 from jax.sharding import PartitionSpec as P
 
 STEP = 10
+
+
+def collect(array, axis, dim):
+    ways = lax.axis_size(axis)
+    up = [(d, (d + 1) % ways) for d in range(ways)]
+    down = [(d, (d - 1) % ways) for d in range(ways)]
+    earlier, later = ([array], [array])
+    for _ in range(ways // 2):
+        earlier.append(lax.ppermute(earlier[-1], axis, up))
+    for _ in range((ways - 1) // 2):
+        later.append(lax.ppermute(later[-1], axis, down))
+    line = jnp.concatenate([*earlier[::-1], *later[1:]], axis=dim)
+    return jnp.roll(line, (lax.axis_index(axis) - ways // 2) * array.shape[dim], axis=dim)
 
 
 def adam_step(low_rank, moment, second):
@@ -19,9 +32,7 @@
 
 def local(inputs, grad_out, projection, moment, second):
     projected = jnp.dot(
-        inputs,
-        lax.all_gather(projection, "fsdp", axis=0, tiled=True),
-        preferred_element_type=jnp.float32,
+        inputs, collect(projection, "fsdp", 0), preferred_element_type=jnp.float32
     ).astype(jnp.bfloat16)
     contract = (((0,), (0,)), ((), ()))
     whole = lax.dot_general(grad_out, projected, contract, preferred_element_type=jnp.float32)

time: 253 us -> 283 us (1.12)
  starting transfers between devices: 0.16 us -> 31.9 us
  waiting for transfers between devices: 209 us -> 186 us
  local copies, waits for them, and re-layouts: 12.5 us -> 33.2 us
    all_gather x1 -> x0, waiting for transfers between devices: 42.8 us -> none  [local(): lax.all_gather(projection, 'fsdp', axis=0, tiled=True)]
    ppermute x0 -> x15, starting transfers between devices: none -> 31.8 us  [the longest x7 31.2 us: collect(): later.append(lax.ppermute(later[-1], axis, down))]
    ppermute x0 -> x15, waiting for transfers between devices: none -> 20.6 us  [the longest x8 19.5 us: collect(): earlier.append(lax.ppermute(earlier[-1], axis, up))]
    unnamed x13 -> x44, local copies, waits for them, and re-layouts: 12.5 us -> 32.6 us
  transfers between devices with their start and end apart: 4 -> 18, of which waited for: 4 -> 17; matrix products, arithmetic and copies ran while one was open for 1% -> 4% of each run, Pallas kernels for 0% -> 0%
where the time goes in v1:
time: 283 us; the launch traced here: 282 us
  waiting for transfers between devices  186 us (66%)
  local copies, waits for them, and re-layouts  33.2 us (12%)
  starting transfers between devices  31.9 us (11%)
  matrix products  15.5 us (5%)
  between operations  13.8 us (5%)
    reduce_scatter x1, waiting for transfers between devices, local(): low_rank = lax.psum_scatter(whole, 'fsdp', scatter_dimension=0, tiled=True)  89.6 us
    all_gather x1, waiting for transfers between devices, local(): lax.all_gather(normalized, 'fsdp', axis=0, tiled=True)  46.6 us
    unnamed x44, local copies, waits for them, and re-layouts  32.6 us
    ppermute x7, starting transfers between devices, collect(): later.append(lax.ppermute(later[-1], axis, down))  31.2 us
    psum x1, waiting for transfers between devices, local(): whole = lax.psum(whole, 'dp')  28.8 us
    ppermute x8, waiting for transfers between devices, collect(): earlier.append(lax.ppermute(earlier[-1], axis, up))  19.5 us
    dot_general x1, matrix products, local(): lax.dot_general(grad_out, projected, contract, preferred_element_type=jnp...  8.41 us
    dot_general x1, matrix products, local(): lax.dot_general(projection, lax.all_gather(normalized, 'fsdp', axis=0, ti...  7.08 us
  transfers between devices with their start and end apart: 18, of which 17 were waited for; matrix products, arithmetic and copies ran while one was open for 4% of the time, Pallas kernels for 0%

profile of v1, /device:TPU:0, one launch (start us, length us, event | category | flops | bytes accessed | tf_op | source)
XLA Modules:
  0.0 282.0 jit_solution(16146803880195846584)
XLA Ops:
  7.8 7.1 %collective-permute-done = bf16[256,128]{1,0:T(8,128)(2,1)S(1)} collective-permute-done((bf16[256,128]{1,0:T(8,128)(2,1)}, bf16[256,128]{1,0:T(8,128)(2,1)S(1)}, u32[]{:S(2)}, u32[]{:S(2)}) %collective-permute-start) | collective-permute-done | bytes 65568 | tf_op jit(solution)/shard_map/ppermute | solution.py:15
  14.9 4.4 %collective-permute-start.8 = (bf16[256,128]{1,0:T(8,128)(2,1)}, bf16[256,128]{1,0:T(8,128)(2,1)S(1)}, u32[]{:S(2)}, u32[]{:S(2)}) collective-permute-start(bf16[256,128]{1,0:T(8,128)(2,1)} %param.7), channel_id=1, source_target_pairs={{0,30},{2,0},{4,2},{6,4},{8,6},{10,8},{12,10},{14,12},{16,14},{18,... | collective-permute-start | bytes 196616 | tf_op jit(solution)/shard_map/ppermute | solution.py:17
  19.3 1.9 collective-permute-done.1
  21.6 4.4 %collective-permute-start.9 = (bf16[256,128]{1,0:T(8,128)(2,1)S(1)}, bf16[256,128]{1,0:T(8,128)(2,1)S(1)}, u32[]{:S(2)}, u32[]{:S(2)}) collective-permute-start(bf16[256,128]{1,0:T(8,128)(2,1)S(1)} %collective-permute-done.8), channel_id=1, source_target_pairs={{0,30},{2,0},{4,2},{6,4},{8,6},{10,8},{12,10},{14,12},{16,14},{18,... | collective-permute-start | bytes 196616 | tf_op jit(solution)/shard_map/ppermute | solution.py:17
  25.9 1.7 collective-permute-done.2
  27.8 4.5 %collective-permute-start.10 = (bf16[256,128]{1,0:T(8,128)(2,1)S(1)}, bf16[256,128]{1,0:T(8,128)(2,1)S(1)}, u32[]{:S(2)}, u32[]{:S(2)}) collective-permute-start(bf16[256,128]{1,0:T(8,128)(2,1)S(1)} %collective-permute-done.9), channel_id=1, source_target_pairs={{0,30},{2,0},{4,2},{6,4},{8,6},{10,8},{12,10},{14,12},{16,14},{18,... | collective-permute-start | bytes 196616 | tf_op jit(solution)/shard_map/ppermute | solution.py:17
  32.3 1.7 collective-permute-done.3
  34.2 4.5 %collective-permute-start.11 = (bf16[256,128]{1,0:T(8,128)(2,1)S(1)}, bf16[256,128]{1,0:T(8,128)(2,1)S(1)}, u32[]{:S(2)}, u32[]{:S(2)}) collective-permute-start(bf16[256,128]{1,0:T(8,128)(2,1)S(1)} %collective-permute-done.10), channel_id=1, source_target_pairs={{0,30},{2,0},{4,2},{6,4},{8,6},{10,8},{12,10},{14,12},{16,14},{18,... | collective-permute-start | bytes 196616 | tf_op jit(solution)/shard_map/ppermute | solution.py:17
  38.7 1.7 collective-permute-done.4
  40.6 4.5 %collective-permute-start.12 = (bf16[256,128]{1,0:T(8,128)(2,1)S(1)}, bf16[256,128]{1,0:T(8,128)(2,1)S(1)}, u32[]{:S(2)}, u32[]{:S(2)}) collective-permute-start(bf16[256,128]{1,0:T(8,128)(2,1)S(1)} %collective-permute-done.11), channel_id=1, source_target_pairs={{0,30},{2,0},{4,2},{6,4},{8,6},{10,8},{12,10},{14,12},{16,14},{18,... | collective-permute-start | bytes 196616 | tf_op jit(solution)/shard_map/ppermute | solution.py:17
  45.1 1.7 collective-permute-done.5
  47.0 4.5 %collective-permute-start.13 = (bf16[256,128]{1,0:T(8,128)(2,1)S(1)}, bf16[256,128]{1,0:T(8,128)(2,1)S(1)}, u32[]{:S(2)}, u32[]{:S(2)}) collective-permute-start(bf16[256,128]{1,0:T(8,128)(2,1)S(1)} %collective-permute-done.12), channel_id=1, source_target_pairs={{0,30},{2,0},{4,2},{6,4},{8,6},{10,8},{12,10},{14,12},{16,14},{18,... | collective-permute-start | bytes 196616 | tf_op jit(solution)/shard_map/ppermute | solution.py:17
  51.5 1.7 collective-permute-done.6
  53.4 4.5 %collective-permute-start.14 = (bf16[256,128]{1,0:T(8,128)(2,1)S(1)}, bf16[256,128]{1,0:T(8,128)(2,1)S(1)}, u32[]{:S(2)}, u32[]{:S(2)}) collective-permute-start(bf16[256,128]{1,0:T(8,128)(2,1)S(1)} %collective-permute-done.13), channel_id=1, source_target_pairs={{0,30},{2,0},{4,2},{6,4},{8,6},{10,8},{12,10},{14,12},{16,14},{18,... | collective-permute-start | bytes 196616 | tf_op jit(solution)/shard_map/ppermute | solution.py:17
  57.9 1.7 collective-permute-done.7
  64.6 1.5 constant_dynamic-update-slice_fusion.23
  80.4 8.4 %convolution_bitcast_fusion = f32[14336,128]{0,1:T(8,128)} fusion(bf16[192,14336]{1,0:T(8,128)(2,1)} %param.6, bf16[192,4096]{1,0:T(8,128)(2,1)S(1)} %copy-done, bf16[8192,128]{1,0:T(8,128)(2,1)} %constant_dynamic-update-slice_fusion, s32[]{:T(128)S(6)} %select_n.14), kind=kOutput, calls=%fused_computation.2 | convolution fusion | flops 905994240 | bytes 15466500 | tf_op jit(solution)/shard_map/dot_general | solution.py:38
  88.9 89.6 %reduce-scatter.2.cloned.1.call-done = f32[896,128]{0,1:T(8,128)} async-done(((f32[14336,128]{0,1:T(8,128)}), f32[896,128]{0,1:T(8,128)}) %reduce-scatter.2.cloned.1.call-update) | async-done | bytes 458768 | tf_op jit(solution)/shard_map/reduce_scatter | solution.py:40
  178.9 28.8 %all-reduce.2.cloned.1.call-done = f32[896,128]{0,1:T(8,128)} async-done(((f32[896,128]{0,1:T(8,128)}), f32[896,128]{0,1:T(8,128)}) %all-reduce.2.cloned.1.call-update) | async-done | bytes 458768 | tf_op jit(solution)/shard_map/psum | solution.py:39
  207.8 2.0 divide_convert_fusion
  209.8 1.0 copy.11
  211.7 46.6 %all-gather.2.cloned.1.call-done = bf16[14336,128]{0,1:T(8,128)(2,1)} async-done(((bf16[896,128]{0,1:T(8,128)(2,1)}), bf16[14336,128]{0,1:T(8,128)(2,1)}) %all-gather.2.cloned.1.call-update) | async-done | bytes 3670032 | tf_op jit(solution)/shard_map/all_gather | solution.py:45
  258.3 7.1 %fusion = bf16[256,14336]{0,1:T(8,128)(2,1)} fusion(bf16[14336,128]{0,1:T(8,128)(2,1)} %all-gather.2.cloned.1.call-done, bf16[256,128]{1,0:T(8,128)(2,1)S(1)} %copy-done.1), kind=kOutput, calls=%fused_computation.1 | convolution fusion | flops 943194112 | bytes 11075584 | tf_op jit(solution)/shard_map/dot_general | solution.py:43
  265.4 10.1 %copy.10 = bf16[256,14336]{1,0:T(8,128)(2,1)} copy(bf16[256,14336]{0,1:T(8,128)(2,1)} %fusion) | data formatting | bytes 14680064
  (63 shorter events, 22.5 us)
Async XLA Ops:
  7.2 73.2 %copy-start = (bf16[192,4096]{1,0:T(8,128)(2,1)S(1)}, bf16[192,4096]{1,0:T(8,128)(2,1)}, u32[]{:S(2)}) copy-start(bf16[192,4096]{1,0:T(8,128)(2,1)} %param.5) | copy-start | bytes 4718596
  7.2 68.2 %copy-start.1 = (bf16[256,128]{1,0:T(8,128)(2,1)S(1)}, bf16[256,128]{1,0:T(8,128)(2,1)}, u32[]{:S(2)}) copy-start(bf16[256,128]{1,0:T(8,128)(2,1)} %param.7) | copy-start | bytes 196612
  7.2 171.3 %reduce-scatter.2.cloned.1.call-start = ((), (), s32[]{:S(2)}) async-start(), calls=%async_computation.2 | async-start | bytes 7798784 | tf_op jit(solution)/shard_map/reduce_scatter | solution.py:40
  7.2 7.7 %collective-permute-start = (bf16[256,128]{1,0:T(8,128)(2,1)}, bf16[256,128]{1,0:T(8,128)(2,1)S(1)}, u32[]{:S(2)}, u32[]{:S(2)}) collective-permute-start(bf16[256,128]{1,0:T(8,128)(2,1)} %param.7), channel_id=1, source_target_pairs={{0,2},{2,4},{4,6},{6,8},{8,10},{10,12},{12,14},{14,16},{16,18},{18... | collective-permute-start | bytes 196616 | tf_op jit(solution)/shard_map/ppermute | solution.py:15
  14.9 6.4 %collective-permute-start.1 = (bf16[256,128]{1,0:T(8,128)(2,1)S(1)}, bf16[256,128]{1,0:T(8,128)(2,1)S(1)}, u32[]{:S(2)}, u32[]{:S(2)}) collective-permute-start(bf16[256,128]{1,0:T(8,128)(2,1)S(1)} %collective-permute-done), channel_id=1, source_target_pairs={{0,2},{2,4},{4,6},{6,8},{8,10},{10,12},{12,14},{14,16},{16,18},{18... | collective-permute-start | bytes 196616 | tf_op jit(solution)/shard_map/ppermute | solution.py:15
  14.9 6.7 %collective-permute-start.8 = (bf16[256,128]{1,0:T(8,128)(2,1)}, bf16[256,128]{1,0:T(8,128)(2,1)S(1)}, u32[]{:S(2)}, u32[]{:S(2)}) collective-permute-start(bf16[256,128]{1,0:T(8,128)(2,1)} %param.7), channel_id=1, source_target_pairs={{0,30},{2,0},{4,2},{6,4},{8,6},{10,8},{12,10},{14,12},{16,14},{18,... | collective-permute-start | bytes 196616 | tf_op jit(solution)/shard_map/ppermute | solution.py:17
  21.3 6.4 %collective-permute-start.2 = (bf16[256,128]{1,0:T(8,128)(2,1)S(1)}, bf16[256,128]{1,0:T(8,128)(2,1)S(1)}, u32[]{:S(2)}, u32[]{:S(2)}) collective-permute-start(bf16[256,128]{1,0:T(8,128)(2,1)S(1)} %collective-permute-done.1), channel_id=1, source_target_pairs={{0,2},{2,4},{4,6},{6,8},{8,10},{10,12},{12,14},{14,16},{16,18},{18... | collective-permute-start | bytes 196616 | tf_op jit(solution)/shard_map/ppermute | solution.py:15
  21.6 6.3 %collective-permute-start.9 = (bf16[256,128]{1,0:T(8,128)(2,1)S(1)}, bf16[256,128]{1,0:T(8,128)(2,1)S(1)}, u32[]{:S(2)}, u32[]{:S(2)}) collective-permute-start(bf16[256,128]{1,0:T(8,128)(2,1)S(1)} %collective-permute-done.8), channel_id=1, source_target_pairs={{0,30},{2,0},{4,2},{6,4},{8,6},{10,8},{12,10},{14,12},{16,14},{18,... | collective-permute-start | bytes 196616 | tf_op jit(solution)/shard_map/ppermute | solution.py:17
  27.7 6.4 %collective-permute-start.3 = (bf16[256,128]{1,0:T(8,128)(2,1)S(1)}, bf16[256,128]{1,0:T(8,128)(2,1)S(1)}, u32[]{:S(2)}, u32[]{:S(2)}) collective-permute-start(bf16[256,128]{1,0:T(8,128)(2,1)S(1)} %collective-permute-done.2), channel_id=1, source_target_pairs={{0,2},{2,4},{4,6},{6,8},{8,10},{10,12},{12,14},{14,16},{16,18},{18... | collective-permute-start | bytes 196616 | tf_op jit(solution)/shard_map/ppermute | solution.py:15
  27.8 6.4 %collective-permute-start.10 = (bf16[256,128]{1,0:T(8,128)(2,1)S(1)}, bf16[256,128]{1,0:T(8,128)(2,1)S(1)}, u32[]{:S(2)}, u32[]{:S(2)}) collective-permute-start(bf16[256,128]{1,0:T(8,128)(2,1)S(1)} %collective-permute-done.9), channel_id=1, source_target_pairs={{0,30},{2,0},{4,2},{6,4},{8,6},{10,8},{12,10},{14,12},{16,14},{18,... | collective-permute-start | bytes 196616 | tf_op jit(solution)/shard_map/ppermute | solution.py:17
  34.1 6.4 %collective-permute-start.4 = (bf16[256,128]{1,0:T(8,128)(2,1)S(1)}, bf16[256,128]{1,0:T(8,128)(2,1)S(1)}, u32[]{:S(2)}, u32[]{:S(2)}) collective-permute-start(bf16[256,128]{1,0:T(8,128)(2,1)S(1)} %collective-permute-done.3), channel_id=1, source_target_pairs={{0,2},{2,4},{4,6},{6,8},{8,10},{10,12},{12,14},{14,16},{16,18},{18... | collective-permute-start | bytes 196616 | tf_op jit(solution)/shard_map/ppermute | solution.py:15
  34.2 6.4 %collective-permute-start.11 = (bf16[256,128]{1,0:T(8,128)(2,1)S(1)}, bf16[256,128]{1,0:T(8,128)(2,1)S(1)}, u32[]{:S(2)}, u32[]{:S(2)}) collective-permute-start(bf16[256,128]{1,0:T(8,128)(2,1)S(1)} %collective-permute-done.10), channel_id=1, source_target_pairs={{0,30},{2,0},{4,2},{6,4},{8,6},{10,8},{12,10},{14,12},{16,14},{18,... | collective-permute-start | bytes 196616 | tf_op jit(solution)/shard_map/ppermute | solution.py:17
  40.5 6.4 %collective-permute-start.5 = (bf16[256,128]{1,0:T(8,128)(2,1)S(1)}, bf16[256,128]{1,0:T(8,128)(2,1)S(1)}, u32[]{:S(2)}, u32[]{:S(2)}) collective-permute-start(bf16[256,128]{1,0:T(8,128)(2,1)S(1)} %collective-permute-done.4), channel_id=1, source_target_pairs={{0,2},{2,4},{4,6},{6,8},{8,10},{10,12},{12,14},{14,16},{16,18},{18... | collective-permute-start | bytes 196616 | tf_op jit(solution)/shard_map/ppermute | solution.py:15
  40.6 6.4 %collective-permute-start.12 = (bf16[256,128]{1,0:T(8,128)(2,1)S(1)}, bf16[256,128]{1,0:T(8,128)(2,1)S(1)}, u32[]{:S(2)}, u32[]{:S(2)}) collective-permute-start(bf16[256,128]{1,0:T(8,128)(2,1)S(1)} %collective-permute-done.11), channel_id=1, source_target_pairs={{0,30},{2,0},{4,2},{6,4},{8,6},{10,8},{12,10},{14,12},{16,14},{18,... | collective-permute-start | bytes 196616 | tf_op jit(solution)/shard_map/ppermute | solution.py:17
  46.8 6.4 %collective-permute-start.6 = (bf16[256,128]{1,0:T(8,128)(2,1)S(1)}, bf16[256,128]{1,0:T(8,128)(2,1)S(1)}, u32[]{:S(2)}, u32[]{:S(2)}) collective-permute-start(bf16[256,128]{1,0:T(8,128)(2,1)S(1)} %collective-permute-done.5), channel_id=1, source_target_pairs={{0,2},{2,4},{4,6},{6,8},{8,10},{10,12},{12,14},{14,16},{16,18},{18... | collective-permute-start | bytes 196616 | tf_op jit(solution)/shard_map/ppermute | solution.py:15
  47.0 6.4 %collective-permute-start.13 = (bf16[256,128]{1,0:T(8,128)(2,1)S(1)}, bf16[256,128]{1,0:T(8,128)(2,1)S(1)}, u32[]{:S(2)}, u32[]{:S(2)}) collective-permute-start(bf16[256,128]{1,0:T(8,128)(2,1)S(1)} %collective-permute-done.12), channel_id=1, source_target_pairs={{0,30},{2,0},{4,2},{6,4},{8,6},{10,8},{12,10},{14,12},{16,14},{18,... | collective-permute-start | bytes 196616 | tf_op jit(solution)/shard_map/ppermute | solution.py:17
  53.2 6.4 %collective-permute-start.7 = (bf16[256,128]{1,0:T(8,128)(2,1)S(1)}, bf16[256,128]{1,0:T(8,128)(2,1)S(1)}, u32[]{:S(2)}, u32[]{:S(2)}) collective-permute-start(bf16[256,128]{1,0:T(8,128)(2,1)S(1)} %collective-permute-done.6), channel_id=1, source_target_pairs={{0,2},{2,4},{4,6},{6,8},{8,10},{10,12},{12,14},{14,16},{16,18},{18... | collective-permute-start | bytes 196616 | tf_op jit(solution)/shard_map/ppermute | solution.py:15
  53.4 16.4 %collective-permute-start.14 = (bf16[256,128]{1,0:T(8,128)(2,1)S(1)}, bf16[256,128]{1,0:T(8,128)(2,1)S(1)}, u32[]{:S(2)}, u32[]{:S(2)}) collective-permute-start(bf16[256,128]{1,0:T(8,128)(2,1)S(1)} %collective-permute-done.13), channel_id=1, source_target_pairs={{0,30},{2,0},{4,2},{6,4},{8,6},{10,8},{12,10},{14,12},{16,14},{18,... | collective-permute-start | bytes 196616 | tf_op jit(solution)/shard_map/ppermute | solution.py:17
  88.8 89.7 %copy-start.2 = (f32[896,128]{1,0:T(8,128)S(1)}, f32[896,128]{1,0:T(8,128)}, u32[]{:S(2)}) copy-start(f32[896,128]{1,0:T(8,128)} %param.8) | copy-start | bytes 1376260
  88.8 89.9 %copy-start.3 = (f32[896,128]{1,0:T(8,128)S(1)}, f32[896,128]{1,0:T(8,128)}, u32[]{:S(2)}) copy-start(f32[896,128]{1,0:T(8,128)} %param.9) | copy-start | bytes 1376260
  88.8 118.9 %all-reduce.2.cloned.1.call-start = ((), (), s32[]{:S(2)}) async-start(), calls=%async_computation.3 | async-start | bytes 917504 | tf_op jit(solution)/shard_map/psum | solution.py:39
  178.5 79.8 %all-gather.2.cloned.1.call-start = ((), (), s32[]{:S(2)}) async-start(), calls=%async_computation.1 | async-start | bytes 3899392 | tf_op jit(solution)/shard_map/all_gather | solution.py:45
Sparse Core Ops, SparseCore 0:
  89.0 89.4 reduce-scatter.1
  180.7 26.9 all-reduce.1
  210.5 47.7 all-gather.1
